TPU v7x, 32 devices: a whole 2x2x4 slice. The times are simulated.
32 devices in a mesh: row: 16 (over z, y, x), col: 2 (over core).
Axes of the slice: x: 2, y: 2, z: 4, core: 2. Of those that a mesh axis runs over, the one named last changes fastest.
Arguments:
- omega_tiles: float32 [128, 24, 128, 128], P('row', 'col'), may hold values from -0.3 to 0.3
- omega_diag: float32 [16384, 128], P(('row', 'col')), may hold values from -0.25 to 2, as said below
- samples: float32 [16384, 128], P(('row', 'col')), may hold values from -6 to 6
- pattern: int32 [128, 24], P('row', 'col'), may hold values from 0 to 127, as said below
Outputs:
- next_tiles: float32 [128, 24, 128, 128], P('row', 'col')
- next_diag: float32 [16384, 128], P(('row', 'col'))
Inputs may be any that keep to these rules, and one draw needn't show every extreme that they name: `pattern`: block j stands at slot s of block row i exactly when block i stands at slot s of block row j, and never in the same group of 8 block rows as i. For the block rows of one index of row and the 12 slots of one index of col, at most 8 listed blocks fall in the block rows of any one other index of row, and exactly 8 for some. A block may stand at more than one slot of a row. `omega_diag`: each row's entry on the diagonal of its block lies in 1 to 2; the others lie within -0.25 to 0.25.
All inputs are finite; a program needn't handle non-finite values.
Results may differ from a plain program's by a relative error of at most 0.00012.
Values sent between devices are 32-bit elements; how exact they have to be, the bound alone decides.
A program may use at most 128 MiB of HBM per device.

v0:
```python
import jax
import jax.numpy as jnp
from jax import lax
from jax.experimental import pallas as pl
from jax.experimental.pallas import tpu as pltpu
from jax.sharding import PartitionSpec as P

ITERS = 2


step_size = 0.2
shrink_weight = 0.05
ridge_weight = 0.1


def soft_shrink(values, threshold):
    return values - jnp.clip(values, -threshold, threshold)


def listed_sweeps(omega_tiles, omega_diag, samples, pattern):
    highest = lax.Precision.HIGHEST
    row_count = lax.axis_size("row")
    col_count = lax.axis_size("col")
    my_row = lax.axis_index("row")
    my_col = lax.axis_index("col")
    block_rows = omega_tiles.shape[0]
    slot_count = omega_tiles.shape[1]
    block_size = omega_tiles.shape[2]
    sample_count = samples.shape[1]
    diag_blocks = block_rows // col_count
    all_blocks = block_rows * row_count
    peer_span = row_count // 2 - 2
    capacity = max(1, (slot_count * block_rows // 2 - 1 + peer_span - 1) // peer_span)
    tile_count = block_rows * slot_count
    x_rows = lax.all_gather(samples, "col", axis=0, tiled=True)
    x_blocks = x_rows.reshape(block_rows, block_size, sample_count)
    slot_ids = my_col * slot_count + jnp.arange(slot_count, dtype=jnp.int32)
    own_blocks = my_row * block_rows + jnp.arange(block_rows, dtype=jnp.int32)
    peer_row = (pattern // block_rows).reshape(tile_count)
    order_key = (
        slot_ids[None, :] * all_blocks + jnp.minimum(own_blocks[:, None], pattern)
    ).reshape(tile_count)
    same_peer = peer_row[:, None] == peer_row[None, :]
    before = order_key[None, :] < order_key[:, None]
    peer_rank = jnp.sum((same_peer & before).astype(jnp.int32), axis=1)
    dest_slot = peer_row * capacity + peer_rank
    source_row = jnp.arange(tile_count, dtype=jnp.int32) // slot_count

    def pack_slots(values):
        empty_slots = jnp.zeros((row_count * capacity,) + values.shape[1:], jnp.float32)
        return empty_slots.at[dest_slot].set(values)

    def unpack_slots(received):
        return received[dest_slot].reshape((block_rows, slot_count) + received.shape[1:])

    x_tiles = unpack_slots(
        lax.all_to_all(
            pack_slots(x_blocks[source_row]), "row", split_axis=0, concat_axis=0, tiled=True
        )
    )
    first_diag = my_col * diag_blocks
    x_diag = lax.dynamic_slice_in_dim(x_blocks, first_diag, diag_blocks, 0)
    identity = jnp.eye(block_size, dtype=jnp.float32)
    tile_vals = omega_tiles
    diag_vals = omega_diag.reshape(diag_blocks, block_size, block_size)
    for sweep_index in range(ITERS):
        row_terms = jnp.einsum("askm,asmn->akn", tile_vals, x_tiles, precision=highest)
        diag_terms = jnp.einsum("bkm,bmn->bkn", diag_vals, x_diag, precision=highest)
        own_terms = lax.dynamic_slice_in_dim(row_terms, first_diag, diag_blocks, 0) + diag_terms
        row_terms = lax.dynamic_update_slice_in_dim(row_terms, own_terms, first_diag, 0)
        products = lax.psum(row_terms, "col")
        cross_terms = jnp.einsum("akn,asqn->askq", products, x_tiles, precision=highest)
        returned = lax.all_to_all(
            pack_slots(products[source_row]), "row", split_axis=0, concat_axis=0, tiled=True
        )
        mirror = jnp.einsum("akn,asqn->askq", x_blocks, unpack_slots(returned), precision=highest)
        gradient = (cross_terms + mirror) * (0.5 / sample_count) + ridge_weight * tile_vals
        tile_vals = soft_shrink(tile_vals - step_size * gradient, step_size * shrink_weight)
        y_diag = lax.dynamic_slice_in_dim(products, first_diag, diag_blocks, 0)
        self_cross = jnp.einsum("bkn,bqn->bkq", y_diag, x_diag, precision=highest)
        pivots = jnp.diagonal(diag_vals, axis1=1, axis2=2)
        diag_grad = (self_cross + jnp.swapaxes(self_cross, 1, 2)) * (
            0.5 / sample_count
        ) + ridge_weight * diag_vals
        diag_grad = diag_grad - identity * (1.0 / pivots)[:, :, None]
        stepped = diag_vals - step_size * diag_grad
        diag_vals = identity * stepped + (1.0 - identity) * soft_shrink(
            stepped, step_size * shrink_weight
        )
    return (tile_vals, diag_vals.reshape(omega_diag.shape))


def halves(values):
    high = values.astype(jnp.bfloat16)
    low = (values - high.astype(jnp.float32)).astype(jnp.bfloat16)
    return high, low


def stacked(values):
    return jnp.concatenate(halves(values), axis=0)


def beside(values):
    return jnp.concatenate(halves(values), axis=1)


def fold(full):
    rows, cols = full.shape[0] // 2, full.shape[1] // 2
    return full[:rows, :cols] + (full[:rows, cols:] + full[rows:, :cols])


def times(left, right):
    return jnp.dot(stacked(left), beside(right), preferred_element_type=jnp.float32)


def doubled(values):
    tall = stacked(values)
    return jnp.concatenate([tall, tall], axis=1)


def times_transposed(left_doubled, rights):
    right = jnp.concatenate([beside(r) for r in rights], axis=0)
    full = lax.dot_general(
        left_doubled, right, (((1,), (1,)), ((), ())), preferred_element_type=jnp.float32
    )
    rows, cols = full.shape[0] // 2, rights[0].shape[0]
    full = full[:rows] + full[rows:]
    return [full[:, n * cols : (n + 1) * cols] for n in range(len(rights))]


def product_row(tile_of, x_of, slot_count):
    left = jnp.concatenate([tile_of(s) for s in range(slot_count)], axis=1)
    right = jnp.concatenate([x_of(s) for s in range(slot_count)], axis=0)
    return fold(times(left, right))


def stepped_diag(diag, pair_sum, sample_count):
    size = diag.shape[0]
    on_diagonal = lax.broadcasted_iota(jnp.int32, (size, size), 0) == lax.broadcasted_iota(
        jnp.int32, (size, size), 1
    )
    gradient = pair_sum * (0.5 / sample_count) + ridge_weight * diag
    gradient = gradient - jnp.where(on_diagonal, 1.0 / jnp.where(on_diagonal, diag, 1.0), 0.0)
    stepped = diag - step_size * gradient
    return jnp.where(on_diagonal, stepped, soft_shrink(stepped, step_size * shrink_weight))


MESH = pl.DeviceIdType.MESH
CORNERS = 4
PARTS = 2
SIGNS = (-1, 1)
SLOT_GROUP = 2
WORK_ROWS = 1


class Place:
    def __init__(self):
        self.row = lax.axis_index("row")
        self.col = lax.axis_index("col")
        self.planes = lax.axis_size("row") // CORNERS
        self.z = self.row // CORNERS
        corner = self.row % CORNERS
        y, x = corner // 2, corner % 2
        self.own = y * 2 + x
        self.beside = y * 2 + (1 - x)
        self.across = (1 - y) * 2 + x
        self.opposite = (1 - y) * 2 + (1 - x)

    def at(self, corner):
        return (self.z * CORNERS + corner, self.col)

    def up(self):
        return (self.row + CORNERS, self.col)

    def down(self):
        return (self.row - CORNERS, self.col)

    def partner(self):
        return (self.row, 1 - self.col)

    def in_plane(self, z, origin):
        middle = self.planes // 2
        low = (z < middle) & (origin >= z) & (origin < middle)
        high = (z >= middle) & (origin >= middle) & (origin <= z)
        return low | high


def greet(place):
    barrier = pltpu.get_barrier_semaphore()
    always = (place.at(place.beside), place.at(place.across), place.partner())
    for other in always:
        pl.semaphore_signal(barrier, inc=1, device_id=other, device_id_type=MESH)

    @pl.when(place.z < place.planes - 1)
    def _():
        pl.semaphore_signal(barrier, inc=1, device_id=place.up(), device_id_type=MESH)

    @pl.when(place.z > 0)
    def _():
        pl.semaphore_signal(barrier, inc=1, device_id=place.down(), device_id_type=MESH)

    upper = (place.z < place.planes - 1).astype(jnp.int32)
    lower = (place.z > 0).astype(jnp.int32)
    pl.semaphore_wait(barrier, len(always) + upper + lower)


def gather(place, all_ref, recv, passed, sent, work=()):
    part = all_ref.shape[0] // (place.planes * CORNERS * 2 * PARTS)
    planes, z = place.planes, place.z

    def copy(kind, origin, corner, q, to, col=None):
        source_row = origin * CORNERS + corner
        col = place.col if col is None else col
        first = ((source_row * 2 + col) * PARTS + q) * part
        ref = all_ref.at[pl.ds(first, part)]
        landed = passed if kind == 4 else recv
        return pltpu.make_async_remote_copy(
            src_ref=ref,
            dst_ref=ref,
            send_sem=sent.at[kind, source_row, q],
            recv_sem=landed.at[source_row, q],
            device_id=to,
            device_id_type=MESH,
        )

    def each_origin(distance, act):
        for sign in SIGNS if distance else (0,):
            origin = z + sign * distance

            @pl.when((origin >= 0) & (origin < planes))
            def _(origin=origin, sign=sign):
                act(origin, sign)

    def arrive(origin, corner, q):
        copy(0, origin, corner, q, place.partner()).wait_recv()

    def own_along(distance, do):
        def act(origin, sign):
            for q in range(PARTS):
                if distance and do == "start":
                    arrive(origin, place.own, q)
                if sign <= 0:

                    @pl.when(z < planes - 1)
                    def _():
                        getattr(copy(0, origin, place.own, q, place.up()), do)()

                if sign >= 0:

                    @pl.when(z > 0)
                    def _():
                        getattr(copy(1, origin, place.own, q, place.down()), do)()

                getattr(copy(4, origin, place.own, q, place.partner()), do)()

        each_origin(distance, act)

    def own_plane(distance, do):
        def act(origin, sign):
            for kind, corner, first in ((2, place.beside, 1), (3, place.across, 0)):
                for q in [p for p in range(PARTS) if p % 2 == first] + [
                    p for p in range(PARTS) if p % 2 != first
                ]:
                    getattr(copy(kind, origin, place.own, q, place.at(corner)), do)()

        each_origin(distance, act)

    def near(distance, do, within):
        def act(origin, sign):
            @pl.when(place.in_plane(z, origin) == within)
            def _():
                relay(origin)

        def relay(origin):
            sides = ((0, place.beside, 3, place.across), (1, place.across, 2, place.beside))
            for relayed in (True, False):
                for side, corner, kind, to in sides:
                    for q in range(PARTS):
                        if (side == q % 2) != relayed:
                            continue
                        if do == "start":
                            arrive(origin, corner, q)
                        if relayed and within:
                            getattr(copy(kind, origin, corner, q, place.at(to)), do)()

                        getattr(copy(4, origin, corner, q, place.partner()), do)()

        each_origin(distance, act)

    def far(distance, do, within):
        def act(origin, sign):
            @pl.when(place.in_plane(z, origin) == within)
            def _():
                for q in range(PARTS):
                    if do == "start":
                        arrive(origin, place.opposite, q)
                    if sign <= 0:

                        @pl.when((z < planes - 1) & jnp.logical_not(place.in_plane(z + 1, origin)))
                        def _():
                            getattr(copy(0, origin, place.opposite, q, place.up()), do)()

                    if sign >= 0:

                        @pl.when((z > 0) & jnp.logical_not(place.in_plane(z - 1, origin)))
                        def _():
                            getattr(copy(1, origin, place.opposite, q, place.down()), do)()

                    getattr(copy(4, origin, place.opposite, q, place.partner()), do)()

        each_origin(distance, act)

    steps = [(own_along, 0), (own_plane, 0)]
    for distance in range(planes):
        if distance + 1 < planes:
            steps += [(own_along, distance + 1)]
        if distance == 0:
            steps += [(near, 0, True), (own_plane, 1), (far, 0, True)]
        else:
            if distance + 1 < planes:
                steps += [(own_plane, distance + 1)]
                steps += [(far, distance, False), (near, distance, True)]
    for distance in range(1, planes):
        steps += [(near, distance, False), (far, distance, True)]
        if distance + 1 == planes:
            steps += [(near, distance, True), (far, distance, False)]

    def passed_on(origin, corner):
        for q in range(PARTS):
            copy(4, origin, corner, q, place.partner(), 1 - place.col).wait_recv()

    def run(do):
        pending = list(work)
        for count, step in enumerate(steps):
            step[0](step[1], do, *step[2:])
            if do == "start" and count == 2:
                passed_on(z, place.own)
            if do == "start" and count >= 2 and pending:
                pending.pop(0)()
        if do == "start":
            for unit in pending:
                unit()

    run("start")
    run("wait_send")

    @pl.loop(0, planes)
    def _(origin):
        for corner in range(CORNERS):

            @pl.when((origin != z) | (corner != place.own))
            def _():
                passed_on(origin, corner)


def sweeps_kernel(
    pattern,
    tiles_in,
    diag_in,
    samples,
    tiles_out,
    diag_out,
    tiles,
    x_all,
    y_part,
    y_in,
    recv,
    passed,
    sent,
    local,
    pair,
    *y_every,
):
    place = Place()
    block_rows, slot_count = tiles.shape[:2]
    diag_blocks = diag_in.shape[0]
    sample_count = x_all.shape[2]
    first_own = place.row * block_rows
    first_diag = place.col * diag_blocks
    first_other = (1 - place.col) * diag_blocks
    load = pltpu.make_async_copy(tiles_in, tiles, local.at[0])
    load.start()
    mine = pl.ds(first_own + first_diag, diag_blocks)
    take = pltpu.make_async_copy(samples, x_all.at[mine], local.at[1])
    take.start()
    greet(place)
    take.wait()
    gather(place, x_all, recv.at[0], passed.at[0], sent)
    load.wait()

    def y_row(a):
        y_part[a] = product_row(lambda s: tiles[a, s], lambda s: x_all[pattern[a, s]], slot_count)

    def send_partial(sweep):
        return pltpu.make_async_remote_copy(
            src_ref=y_part.at[pl.ds(first_other, diag_blocks)],
            dst_ref=y_in.at[sweep],
            send_sem=pair.at[0, sweep],
            recv_sem=pair.at[1, sweep],
            device_id=place.partner(),
            device_id_type=MESH,
        )

    groups = [
        range(s, min(s + SLOT_GROUP, slot_count)) for s in range(0, slot_count, SLOT_GROUP)
    ]
    pair_weight = step_size * 0.5 / sample_count

    def cross_tiles(a, y_all):
        left = doubled(y_all[first_own + a])
        for group in groups:
            found = times_transposed(left, [x_all[pattern[a, s]] for s in group])
            for s, cross in zip(group, found):
                tiles[a, s] = (1.0 - step_size * ridge_weight) * tiles[a, s] - pair_weight * cross

    def mirror_tiles(a, y_all):
        left = doubled(x_all[first_own + a])
        for group in groups:
            found = times_transposed(left, [y_all[pattern[a, s]] for s in group])
            for s, mirror in zip(group, found):
                tiles[a, s] = soft_shrink(
                    tiles[a, s] - pair_weight * mirror, step_size * shrink_weight
                )

    def step_own(d, y_all, diag):
        own = first_own + first_diag + d
        pair_sum = (
            times_transposed(doubled(y_all[own]), [x_all[own]])[0]
            + times_transposed(doubled(x_all[own]), [y_all[own]])[0]
        )
        diag_out[d] = stepped_diag(diag[d], pair_sum, sample_count)

    def products(sweep, y_all, before, diag):
        @pl.loop(0, diag_blocks)
        def _(d):
            before(first_other + d)
            y_row(first_other + d)

        sending = send_partial(sweep)
        sending.start()

        @pl.loop(0, diag_blocks)
        def _(d):
            before(first_diag + d)
            y_row(first_diag + d)
            y_part[first_diag + d] += fold(times(diag[d], x_all[first_own + first_diag + d]))

        sending.wait()

        @pl.loop(0, diag_blocks)
        def _(d):
            y_all[first_own + first_diag + d] = y_part[first_diag + d] + y_in[sweep, d]

        def unit(first):
            @pl.loop(0, WORK_ROWS)
            def _(n):
                cross_tiles((first_diag + first + n) % block_rows, y_all)

        def unit_diag():
            @pl.loop(0, diag_blocks)
            def _(d):
                step_own(d, y_all, diag)

        work = [lambda first=first: unit(first) for first in range(0, block_rows, WORK_ROWS)]
        work.insert(1, unit_diag)
        gather(place, y_all, recv.at[1 + sweep], passed.at[1 + sweep], sent, work)

    products(0, y_every[0], lambda a: None, diag_in)
    for sweep in range(ITERS - 1):
        products(
            sweep + 1, y_every[sweep + 1], lambda a: mirror_tiles(a, y_every[sweep]), diag_out
        )

    @pl.loop(0, block_rows)
    def _(a):
        mirror_tiles(a, y_every[-1])
        pltpu.make_async_copy(tiles.at[a], tiles_out.at[a], local.at[2 + a]).start()

    @pl.loop(0, block_rows)
    def _(a):
        pltpu.make_async_copy(tiles.at[a], tiles_out.at[a], local.at[2 + a]).wait()


def gathered_sweeps(omega_tiles, omega_diag, samples, pattern):
    block_rows, slot_count, size, _ = omega_tiles.shape
    row_count = lax.axis_size("row")
    sample_count = samples.shape[1]
    diag_blocks = block_rows // lax.axis_size("col")
    diag = omega_diag.reshape(diag_blocks, size, size)
    every = pltpu.VMEM((row_count * block_rows, size, sample_count), jnp.float32)
    in_vmem = pl.BlockSpec(memory_space=pltpu.VMEM)
    anywhere = pl.BlockSpec(memory_space=pl.ANY)
    tiles, diag = pl.pallas_call(
        sweeps_kernel,
        name="sweeps",
        out_shape=[
            jax.ShapeDtypeStruct(omega_tiles.shape, jnp.float32),
            jax.ShapeDtypeStruct(diag.shape, jnp.float32),
        ],
        in_specs=[pl.BlockSpec(memory_space=pltpu.SMEM), anywhere, in_vmem, anywhere],
        out_specs=[anywhere, in_vmem],
        scratch_shapes=[
            pltpu.VMEM(omega_tiles.shape, jnp.float32),
            every,
            pltpu.VMEM((block_rows, size, sample_count), jnp.float32),
            pltpu.VMEM((ITERS, diag_blocks, size, sample_count), jnp.float32),
            pltpu.SemaphoreType.DMA((1 + ITERS, row_count, PARTS)),
            pltpu.SemaphoreType.DMA((1 + ITERS, row_count, PARTS)),
            pltpu.SemaphoreType.DMA((5, row_count, PARTS)),
            pltpu.SemaphoreType.DMA((2 + block_rows,)),
            pltpu.SemaphoreType.DMA((2, ITERS)),
        ]
        + [every] * ITERS,
        compiler_params=pltpu.CompilerParams(
            collective_id=0, has_side_effects=True, vmem_limit_bytes=56 * 2**20
        ),
    )(pattern, omega_tiles, diag, samples.reshape(diag_blocks, size, sample_count))
    return tiles, diag.reshape(omega_diag.shape)


def on_device(omega_tiles, omega_diag, samples, pattern):
    row_count = lax.axis_size("row")
    block_rows, slot_count = omega_tiles.shape[:2]
    peer_span = row_count // 2 - 2
    capacity = max(1, (slot_count * block_rows // 2 - 1 + peer_span - 1) // peer_span)
    whole_gather = 2 * capacity >= block_rows and lax.axis_size("col") == 2 and row_count % 4 == 0
    sweeps = gathered_sweeps if whole_gather else listed_sweeps
    return sweeps(omega_tiles, omega_diag, samples, pattern)


def solution(mesh):
    in_specs = (
        P("row", "col", None, None),
        P(("row", "col"), None),
        P(("row", "col"), None),
        P("row", "col"),
    )
    out_specs = (P("row", "col", None, None), P(("row", "col"), None))
    return jax.shard_map(
        on_device, mesh=mesh, in_specs=in_specs, out_specs=out_specs, check_vma=False
    )
```

profile of v0, /device:TPU:0, one launch (start us, length us, event | category | flops | bytes accessed | tf_op | source)
XLA Modules:
  0.0 132.4 jit_solution(8025446773301240076)
XLA Ops:
  0.6 124.7 %sweeps.1 = (f32[8,12,128,128]{3,2,1,0:T(8,128)}, f32[4,128,128]{2,1,0:T(8,128)}) custom-call(s32[8,12]{1,0:T(8,128)} %pattern.1, f32[8,12,128,128]{3,2,1,0:T(8,128)} %tiles_in.1, f32[4,128,128]{2,1,0:T(8,128)} %bitcast.3, f32[4,128,128]{2,1,0:T(8,128)} %bitcast.4), custom_call_target="tpu_custom_call" | custom-call | tf_op jit(solution)/shard_map/sweeps/pallas_call | solution.py:493
  125.3 0.0 copy-start
  125.3 6.3 %copy.8 = f32[8,12,128,128]{3,2,1,0:T(8,128)} copy(f32[8,12,128,128]{3,2,1,0:T(8,128)} %get-tuple-element.8) | data formatting | bytes 12582912
  131.7 0.0 copy-done
  131.7 0.7 copy.9
Async XLA Ops:
  125.3 6.3 %copy-start = (f32[4,128,128]{2,1,0:T(8,128)S(1)}, f32[4,128,128]{2,1,0:T(8,128)}, u32[]{:S(2)}) copy-start(f32[4,128,128]{2,1,0:T(8,128)} %get-tuple-element.5) | copy-start | bytes 786436
where the time goes:
time: 133 us; the launch traced here: 132 us
  Pallas kernels  125 us (94%)
  local copies, waits for them, and re-layouts  7.03 us (5%)
    pallas_call x1, Pallas kernels, gathered_sweeps(): pl.pallas_call(sweeps_kernel, name='sweeps', out_shape=[jax.ShapeDtypeStr...  125 us
    unnamed x4, local copies, waits for them, and re-layouts  7.03 us

commit v1 on v0

--- a/solution.py
+++ b/solution.py
@@ -353,15 +353,31 @@
                 passed_on(origin, corner)
 
 
+def slot_groups(slot_count):
+    return [range(s, min(s + SLOT_GROUP, slot_count)) for s in range(0, slot_count, SLOT_GROUP)]
+
+
+def mirror_row(a, first_own, pattern, tiles, x_all, y_all, stepped, sample_count):
+    slot_count = tiles.shape[1]
+    pair_weight = step_size * 0.5 / sample_count
+    left = doubled(x_all[first_own + a])
+    for group in slot_groups(slot_count):
+        found = times_transposed(left, [y_all[pattern[a, s]] for s in group])
+        for s, mirror in zip(group, found):
+            stepped[a, s] = soft_shrink(
+                tiles[a, s] - pair_weight * mirror, step_size * shrink_weight
+            )
+
+
 def sweeps_kernel(
     pattern,
     tiles_in,
     diag_in,
     samples,
-    tiles_out,
-    diag_out,
     tiles,
     x_all,
+    y_last,
+    diag,
     y_part,
     y_in,
     recv,
@@ -369,9 +385,10 @@
     sent,
     local,
     pair,
-    *y_every,
+    *y_before,
 ):
     place = Place()
+    y_every = [*y_before, y_last]
     block_rows, slot_count = tiles.shape[:2]
     diag_blocks = diag_in.shape[0]
     sample_count = x_all.shape[2]
@@ -379,14 +396,17 @@
     first_diag = place.col * diag_blocks
     first_other = (1 - place.col) * diag_blocks
     load = pltpu.make_async_copy(tiles_in, tiles, local.at[0])
-    load.start()
+    load_diag = pltpu.make_async_copy(diag_in, diag, local.at[2])
     mine = pl.ds(first_own + first_diag, diag_blocks)
     take = pltpu.make_async_copy(samples, x_all.at[mine], local.at[1])
     take.start()
+    load.start()
+    load_diag.start()
     greet(place)
     take.wait()
     gather(place, x_all, recv.at[0], passed.at[0], sent)
     load.wait()
+    load_diag.wait()
 
     def y_row(a):
         y_part[a] = product_row(lambda s: tiles[a, s], lambda s: x_all[pattern[a, s]], slot_count)
@@ -401,9 +421,7 @@
             device_id_type=MESH,
         )
 
-    groups = [
-        range(s, min(s + SLOT_GROUP, slot_count)) for s in range(0, slot_count, SLOT_GROUP)
-    ]
+    groups = slot_groups(slot_count)
     pair_weight = step_size * 0.5 / sample_count
 
     def cross_tiles(a, y_all):
@@ -414,23 +432,17 @@
                 tiles[a, s] = (1.0 - step_size * ridge_weight) * tiles[a, s] - pair_weight * cross
 
     def mirror_tiles(a, y_all):
-        left = doubled(x_all[first_own + a])
-        for group in groups:
-            found = times_transposed(left, [y_all[pattern[a, s]] for s in group])
-            for s, mirror in zip(group, found):
-                tiles[a, s] = soft_shrink(
-                    tiles[a, s] - pair_weight * mirror, step_size * shrink_weight
-                )
-
-    def step_own(d, y_all, diag):
+        mirror_row(a, first_own, pattern, tiles, x_all, y_all, tiles, sample_count)
+
+    def step_own(d, y_all):
         own = first_own + first_diag + d
         pair_sum = (
             times_transposed(doubled(y_all[own]), [x_all[own]])[0]
             + times_transposed(doubled(x_all[own]), [y_all[own]])[0]
         )
-        diag_out[d] = stepped_diag(diag[d], pair_sum, sample_count)
-
-    def products(sweep, y_all, before, diag):
+        diag[d] = stepped_diag(diag[d], pair_sum, sample_count)
+
+    def products(sweep, y_all, before):
         @pl.loop(0, diag_blocks)
         def _(d):
             before(first_other + d)
@@ -459,26 +471,36 @@
         def unit_diag():
             @pl.loop(0, diag_blocks)
             def _(d):
-                step_own(d, y_all, diag)
+                step_own(d, y_all)
 
         work = [lambda first=first: unit(first) for first in range(0, block_rows, WORK_ROWS)]
         work.insert(1, unit_diag)
         gather(place, y_all, recv.at[1 + sweep], passed.at[1 + sweep], sent, work)
 
-    products(0, y_every[0], lambda a: None, diag_in)
+    products(0, y_every[0], lambda a: None)
     for sweep in range(ITERS - 1):
         products(
-            sweep + 1, y_every[sweep + 1], lambda a: mirror_tiles(a, y_every[sweep]), diag_out
-        )
+            sweep + 1, y_every[sweep + 1], lambda a: mirror_tiles(a, y_every[sweep])
+        )
+
+
+def finish_kernel(pattern, tiles, x_all, y_all, diag_in, tiles_out, diag_out, ready, sems):
+    block_rows, slot_count = tiles.shape[:2]
+    sample_count = x_all.shape[2]
+    first_own = lax.axis_index("row") * block_rows
+    diag_out[...] = diag_in[...]
+
+    def store(a):
+        return pltpu.make_async_copy(ready.at[a], tiles_out.at[a], sems.at[a])
 
     @pl.loop(0, block_rows)
     def _(a):
-        mirror_tiles(a, y_every[-1])
-        pltpu.make_async_copy(tiles.at[a], tiles_out.at[a], local.at[2 + a]).start()
+        mirror_row(a, first_own, pattern, tiles, x_all, y_all, ready, sample_count)
+        store(a).start()
 
     @pl.loop(0, block_rows)
     def _(a):
-        pltpu.make_async_copy(tiles.at[a], tiles_out.at[a], local.at[2 + a]).wait()
+        store(a).wait()
 
 
 def gathered_sweeps(omega_tiles, omega_diag, samples, pattern):
@@ -487,34 +509,57 @@
     sample_count = samples.shape[1]
     diag_blocks = block_rows // lax.axis_size("col")
     diag = omega_diag.reshape(diag_blocks, size, size)
-    every = pltpu.VMEM((row_count * block_rows, size, sample_count), jnp.float32)
+    every = (row_count * block_rows, size, sample_count)
     in_vmem = pl.BlockSpec(memory_space=pltpu.VMEM)
-    anywhere = pl.BlockSpec(memory_space=pl.ANY)
-    tiles, diag = pl.pallas_call(
+    in_hbm = pl.BlockSpec(memory_space=pltpu.HBM)
+    in_smem = pl.BlockSpec(memory_space=pltpu.SMEM)
+    tiles, x_all, y_all, diag = pl.pallas_call(
         sweeps_kernel,
         name="sweeps",
         out_shape=[
-            jax.ShapeDtypeStruct(omega_tiles.shape, jnp.float32),
-            jax.ShapeDtypeStruct(diag.shape, jnp.float32),
+            pltpu.VMEM(omega_tiles.shape, jnp.float32),
+            pltpu.VMEM(every, jnp.float32),
+            pltpu.VMEM(every, jnp.float32),
+            pltpu.VMEM(diag.shape, jnp.float32),
         ],
-        in_specs=[pl.BlockSpec(memory_space=pltpu.SMEM), anywhere, in_vmem, anywhere],
-        out_specs=[anywhere, in_vmem],
+        in_specs=[in_smem, in_hbm, in_hbm, in_hbm],
+        out_specs=[in_vmem] * 4,
         scratch_shapes=[
-            pltpu.VMEM(omega_tiles.shape, jnp.float32),
-            every,
             pltpu.VMEM((block_rows, size, sample_count), jnp.float32),
             pltpu.VMEM((ITERS, diag_blocks, size, sample_count), jnp.float32),
             pltpu.SemaphoreType.DMA((1 + ITERS, row_count, PARTS)),
             pltpu.SemaphoreType.DMA((1 + ITERS, row_count, PARTS)),
             pltpu.SemaphoreType.DMA((5, row_count, PARTS)),
-            pltpu.SemaphoreType.DMA((2 + block_rows,)),
+            pltpu.SemaphoreType.DMA((3,)),
             pltpu.SemaphoreType.DMA((2, ITERS)),
         ]
-        + [every] * ITERS,
+        + [pltpu.VMEM(every, jnp.float32)] * (ITERS - 1),
         compiler_params=pltpu.CompilerParams(
-            collective_id=0, has_side_effects=True, vmem_limit_bytes=56 * 2**20
+            collective_id=0, has_side_effects=True, vmem_limit_bytes=40 * 2**20
         ),
-    )(pattern, omega_tiles, diag, samples.reshape(diag_blocks, size, sample_count))
+    )(
+        pattern,
+        *(
+            pltpu.with_memory_space_constraint(v, pltpu.HBM)
+            for v in (omega_tiles, diag, samples.reshape(diag_blocks, size, sample_count))
+        ),
+    )
+    held = [pltpu.with_memory_space_constraint(v, pltpu.VMEM) for v in (tiles, x_all, y_all, diag)]
+    tiles, diag = pl.pallas_call(
+        finish_kernel,
+        name="finish",
+        out_shape=[
+            jax.ShapeDtypeStruct(omega_tiles.shape, jnp.float32),
+            jax.ShapeDtypeStruct(diag.shape, jnp.float32),
+        ],
+        in_specs=[in_smem] + [in_vmem] * 4,
+        out_specs=[in_hbm, in_vmem],
+        scratch_shapes=[
+            pltpu.VMEM(omega_tiles.shape, jnp.float32),
+            pltpu.SemaphoreType.DMA((block_rows,)),
+        ],
+        compiler_params=pltpu.CompilerParams(vmem_limit_bytes=16 * 2**20),
+    )(pattern, *held)
     return tiles, diag.reshape(omega_diag.shape)
 
 

time: 133 us -> 124 us (0.932)
  local copies, waits for them, and re-layouts: 7.03 us -> 0.01 us
  Pallas kernels: 125 us -> 123 us
    unnamed x4 -> x2, local copies, waits for them, and re-layouts: 7.03 us -> 0.01 us
    pallas_call x1 -> x2, Pallas kernels: 125 us -> 123 us  [the longest x1 118 us: gathered_sweeps(): pl.pallas_call(sweeps_kernel, name='sweeps', out_shape=[pltpu.VMEM(omega_...]
where the time goes in v1:
time: 124 us
  Pallas kernels  123 us (99%)
    pallas_call x1, Pallas kernels, gathered_sweeps(): pl.pallas_call(sweeps_kernel, name='sweeps', out_shape=[pltpu.VMEM(omega_...  118 us
    pallas_call x1, Pallas kernels, gathered_sweeps(): pl.pallas_call(finish_kernel, name='finish', out_shape=[jax.ShapeDtypeStr...  5.64 us

profile of v1, /device:TPU:0, one launch (start us, length us, event | category | flops | bytes accessed | tf_op | source)
XLA Modules:
  0.0 124.1 jit_solution(8704536182658472340)
XLA Ops:
  0.6 0.0 copy-start
  0.6 117.8 %sweeps.1 = (f32[8,12,128,128]{3,2,1,0:T(8,128)S(1)}, f32[128,128,128]{2,1,0:T(8,128)S(1)}, f32[128,128,128]{2,1,0:T(8,128)S(1)}, f32[4,128,128]{2,1,0:T(8,128)S(1)}) custom-call(s32[8,12]{1,0:T(8,128)} %pattern.3, f32[8,12,128,128]{3,2,1,0:T(8,128)} %tiles_in.1, f32[4,128,128]{2,1,0:T(8,128)} %bitcast.3, f32[4,128,128]{2,1,0:T(8,128)} %bitcast.4), custom_call_target="tpu_custom_call" | custom-call | tf_op jit(solution)/shard_map/sweeps/pallas_call | solution.py:516
  118.4 0.0 copy-done
  118.4 5.6 %finish.1 = (f32[8,12,128,128]{3,2,1,0:T(8,128)}, f32[4,128,128]{2,1,0:T(8,128)}) custom-call(s32[8,12]{1,0:T(8,128)S(1)} %copy-done, f32[8,12,128,128]{3,2,1,0:T(8,128)S(1)} %get-tuple-element.8.tiles, f32[128,128,128]{2,1,0:T(8,128)S(1)} %get-tuple-element.9.x_all, f32[128,128,128]{2,1,0:T(8,128)S(1)} %get-tuple-element.10.y_all, ...), custom_call_target="tpu_custom_call" | custom-call | tf_op jit(solution)/shard_map/finish/pallas_call | solution.py:548
Async XLA Ops:
  0.6 117.8 %copy-start = (s32[8,12]{1,0:T(8,128)S(1)}, s32[8,12]{1,0:T(8,128)}, u32[]{:S(2)}) copy-start(s32[8,12]{1,0:T(8,128)} %pattern.3) | copy-start | bytes 1156

commit v2 on v1

--- a/solution.py
+++ b/solution.py
@@ -147,10 +147,13 @@
 
 MESH = pl.DeviceIdType.MESH
 CORNERS = 4
-PARTS = 2
-SIGNS = (-1, 1)
 SLOT_GROUP = 2
-WORK_ROWS = 1
+SEND_US = 1.44
+HOP_US = 1.7
+LEAD_US = 1.5
+ROW_US = (0.55, 1.1)
+UNIT_US = 1.44
+INNER, OUTER, ACROSS_X, ACROSS_Y, PARTNER = range(5)
 
 
 class Place:
@@ -158,199 +161,201 @@
         self.row = lax.axis_index("row")
         self.col = lax.axis_index("col")
         self.planes = lax.axis_size("row") // CORNERS
-        self.z = self.row // CORNERS
+        z = self.row // CORNERS
         corner = self.row % CORNERS
         y, x = corner // 2, corner % 2
-        self.own = y * 2 + x
-        self.beside = y * 2 + (1 - x)
-        self.across = (1 - y) * 2 + x
-        self.opposite = (1 - y) * 2 + (1 - x)
-
-    def at(self, corner):
-        return (self.z * CORNERS + corner, self.col)
-
-    def up(self):
-        return (self.row + CORNERS, self.col)
-
-    def down(self):
-        return (self.row - CORNERS, self.col)
-
-    def partner(self):
-        return (self.row, 1 - self.col)
-
-    def in_plane(self, z, origin):
-        middle = self.planes // 2
-        low = (z < middle) & (origin >= z) & (origin < middle)
-        high = (z >= middle) & (origin >= middle) & (origin <= z)
-        return low | high
-
-
-def greet(place):
-    barrier = pltpu.get_barrier_semaphore()
-    always = (place.at(place.beside), place.at(place.across), place.partner())
-    for other in always:
-        pl.semaphore_signal(barrier, inc=1, device_id=other, device_id_type=MESH)
-
-    @pl.when(place.z < place.planes - 1)
-    def _():
-        pl.semaphore_signal(barrier, inc=1, device_id=place.up(), device_id_type=MESH)
-
-    @pl.when(place.z > 0)
-    def _():
-        pl.semaphore_signal(barrier, inc=1, device_id=place.down(), device_id_type=MESH)
-
-    upper = (place.z < place.planes - 1).astype(jnp.int32)
-    lower = (place.z > 0).astype(jnp.int32)
-    pl.semaphore_wait(barrier, len(always) + upper + lower)
-
-
-def gather(place, all_ref, recv, passed, sent, work=()):
-    part = all_ref.shape[0] // (place.planes * CORNERS * 2 * PARTS)
-    planes, z = place.planes, place.z
-
-    def copy(kind, origin, corner, q, to, col=None):
-        source_row = origin * CORNERS + corner
-        col = place.col if col is None else col
-        first = ((source_row * 2 + col) * PARTS + q) * part
-        ref = all_ref.at[pl.ds(first, part)]
-        landed = passed if kind == 4 else recv
+        upper = (z >= self.planes // 2).astype(jnp.int32)
+        self.sign = 1 - 2 * upper
+        self.base = upper * (self.planes - 1)
+        self.plane = self.base + self.sign * z
+        self.corners = {
+            "own": corner,
+            "beside": y * 2 + (1 - x),
+            "across": (1 - y) * 2 + x,
+            "opposite": (1 - y) * 2 + (1 - x),
+        }
+        first = z * CORNERS
+        self.target = {
+            INNER: (self.row + CORNERS * self.sign, self.col),
+            OUTER: (self.row - CORNERS * self.sign, self.col),
+            ACROSS_X: (first + self.corners["beside"], self.col),
+            ACROSS_Y: (first + self.corners["across"], self.col),
+            PARTNER: (self.row, 1 - self.col),
+        }
+
+    def source(self, origin, corner):
+        return (self.base + self.sign * origin) * CORNERS + self.corners[corner]
+
+
+def in_plane(planes, plane, origin):
+    middle = planes // 2
+    if plane < middle:
+        return plane <= origin < middle
+    return middle <= origin <= plane
+
+
+def onward(planes, plane, origin, corner, part):
+    found = []
+    rising = origin <= plane < planes - 1
+    falling = origin >= plane > 0
+    if corner == "own":
+        if rising:
+            found.append((INNER, plane + 1, "own"))
+        if falling:
+            found.append((OUTER, plane - 1, "own"))
+        found += [(ACROSS_X, plane, "beside"), (ACROSS_Y, plane, "across")]
+    elif corner == "beside":
+        if in_plane(planes, plane, origin) and part % 2 == 1:
+            found.append((ACROSS_Y, plane, "opposite"))
+    elif corner == "across":
+        if in_plane(planes, plane, origin) and part % 2 == 0:
+            found.append((ACROSS_X, plane, "opposite"))
+    else:
+        if rising and not in_plane(planes, plane + 1, origin):
+            found.append((INNER, plane + 1, "opposite"))
+        if falling and not in_plane(planes, plane - 1, origin):
+            found.append((OUTER, plane - 1, "opposite"))
+    return found
+
+
+def plan(planes, ready):
+    parts = len(ready)
+    waiting = {}
+    free_at = {}
+    acts = [[] for _ in range(planes)]
+    events = []
+    count = 0
+    for plane in range(planes):
+        for q in range(parts):
+            events.append((ready[q], count, plane, (plane, "own", q), None))
+            count += 1
+    while events:
+        event = min(events)
+        events.remove(event)
+        now, _, plane, part, link = event
+        touched = []
+        if link is None:
+            origin, corner, q = part
+            if (origin, corner) != (plane, "own"):
+                acts[plane].append((now, "take", part))
+            for out, _, _ in onward(planes, plane, origin, corner, q):
+                waiting.setdefault((plane, out), []).append(
+                    (abs(plane - origin), now, count, part)
+                )
+                count += 1
+                touched.append((plane, out))
+        else:
+            touched.append((plane, link))
+        for key in touched:
+            queue = waiting.get(key, [])
+            if not queue or free_at.get(key, -1.0) > now:
+                continue
+            item = min(queue)
+            queue.remove(item)
+            free_at[key] = now + SEND_US
+            events.append((now + SEND_US, count, plane, None, key[1]))
+            count += 1
+            sent = item[3]
+            if sent[:2] != (plane, "own"):
+                acts[plane].append((max(item[1], now - LEAD_US) + 1e-6, "send", key[1], sent))
+            for out, to, corner in onward(planes, plane, *sent):
+                if out == key[1]:
+                    events.append(
+                        (now + SEND_US + HOP_US, count, to, (sent[0], corner, sent[2]), None)
+                    )
+                    count += 1
+    return [sorted(found, key=lambda act: act[0]) for found in acts]
+
+
+class Gather:
+    def __init__(self, place, all_ref, parts, recv, passed, met, sent, ready):
+        self.place, self.all_ref, self.parts = place, all_ref, parts
+        self.recv, self.passed, self.met, self.sent = recv, passed, met, sent
+        self.size = all_ref.shape[0] // (place.planes * CORNERS * 2 * parts)
+        self.near = range((place.planes + 1) // 2)
+        self.acts = plan(place.planes, ready)
+
+    def copy(self, link, part, col=None):
+        origin, corner, q = part
+        row = self.place.source(origin, corner)
+        col = self.place.col if col is None else col
+        ref = self.all_ref.at[pl.ds(((row * 2 + col) * self.parts + q) * self.size, self.size)]
+        landed = self.recv.at[row, q] if link != PARTNER else self.passed
+        return self.describe(ref, link, landed)
+
+    def describe(self, ref, link, landed):
         return pltpu.make_async_remote_copy(
             src_ref=ref,
             dst_ref=ref,
-            send_sem=sent.at[kind, source_row, q],
-            recv_sem=landed.at[source_row, q],
-            device_id=to,
+            send_sem=self.sent.at[link],
+            recv_sem=landed,
+            device_id=self.place.target[link],
             device_id_type=MESH,
         )
 
-    def each_origin(distance, act):
-        for sign in SIGNS if distance else (0,):
-            origin = z + sign * distance
-
-            @pl.when((origin >= 0) & (origin < planes))
-            def _(origin=origin, sign=sign):
-                act(origin, sign)
-
-    def arrive(origin, corner, q):
-        copy(0, origin, corner, q, place.partner()).wait_recv()
-
-    def own_along(distance, do):
-        def act(origin, sign):
-            for q in range(PARTS):
-                if distance and do == "start":
-                    arrive(origin, place.own, q)
-                if sign <= 0:
-
-                    @pl.when(z < planes - 1)
-                    def _():
-                        getattr(copy(0, origin, place.own, q, place.up()), do)()
-
-                if sign >= 0:
-
-                    @pl.when(z > 0)
-                    def _():
-                        getattr(copy(1, origin, place.own, q, place.down()), do)()
-
-                getattr(copy(4, origin, place.own, q, place.partner()), do)()
-
-        each_origin(distance, act)
-
-    def own_plane(distance, do):
-        def act(origin, sign):
-            for kind, corner, first in ((2, place.beside, 1), (3, place.across, 0)):
-                for q in [p for p in range(PARTS) if p % 2 == first] + [
-                    p for p in range(PARTS) if p % 2 != first
-                ]:
-                    getattr(copy(kind, origin, place.own, q, place.at(corner)), do)()
-
-        each_origin(distance, act)
-
-    def near(distance, do, within):
-        def act(origin, sign):
-            @pl.when(place.in_plane(z, origin) == within)
-            def _():
-                relay(origin)
-
-        def relay(origin):
-            sides = ((0, place.beside, 3, place.across), (1, place.across, 2, place.beside))
-            for relayed in (True, False):
-                for side, corner, kind, to in sides:
-                    for q in range(PARTS):
-                        if (side == q % 2) != relayed:
-                            continue
-                        if do == "start":
-                            arrive(origin, corner, q)
-                        if relayed and within:
-                            getattr(copy(kind, origin, corner, q, place.at(to)), do)()
-
-                        getattr(copy(4, origin, corner, q, place.partner()), do)()
-
-        each_origin(distance, act)
-
-    def far(distance, do, within):
-        def act(origin, sign):
-            @pl.when(place.in_plane(z, origin) == within)
-            def _():
-                for q in range(PARTS):
-                    if do == "start":
-                        arrive(origin, place.opposite, q)
-                    if sign <= 0:
-
-                        @pl.when((z < planes - 1) & jnp.logical_not(place.in_plane(z + 1, origin)))
-                        def _():
-                            getattr(copy(0, origin, place.opposite, q, place.up()), do)()
-
-                    if sign >= 0:
-
-                        @pl.when((z > 0) & jnp.logical_not(place.in_plane(z - 1, origin)))
-                        def _():
-                            getattr(copy(1, origin, place.opposite, q, place.down()), do)()
-
-                    getattr(copy(4, origin, place.opposite, q, place.partner()), do)()
-
-        each_origin(distance, act)
-
-    steps = [(own_along, 0), (own_plane, 0)]
-    for distance in range(planes):
-        if distance + 1 < planes:
-            steps += [(own_along, distance + 1)]
-        if distance == 0:
-            steps += [(near, 0, True), (own_plane, 1), (far, 0, True)]
-        else:
-            if distance + 1 < planes:
-                steps += [(own_plane, distance + 1)]
-                steps += [(far, distance, False), (near, distance, True)]
-    for distance in range(1, planes):
-        steps += [(near, distance, False), (far, distance, True)]
-        if distance + 1 == planes:
-            steps += [(near, distance, True), (far, distance, False)]
-
-    def passed_on(origin, corner):
-        for q in range(PARTS):
-            copy(4, origin, corner, q, place.partner(), 1 - place.col).wait_recv()
-
-    def run(do):
-        pending = list(work)
-        for count, step in enumerate(steps):
-            step[0](step[1], do, *step[2:])
-            if do == "start" and count == 2:
-                passed_on(z, place.own)
-            if do == "start" and count >= 2 and pending:
-                pending.pop(0)()
-        if do == "start":
-            for unit in pending:
-                unit()
-
-    run("start")
-    run("wait_send")
-
-    @pl.loop(0, planes)
-    def _(origin):
-        for corner in range(CORNERS):
-
-            @pl.when((origin != z) | (corner != place.own))
-            def _():
-                passed_on(origin, corner)
+    def own(self, q, col=None):
+        col = self.place.col if col is None else col
+        first = ((self.place.row * 2 + col) * self.parts + q) * self.size
+        return self.all_ref.at[pl.ds(first, self.size)]
+
+    def start_own(self, q):
+        ref = self.own(q)
+        for link in (ACROSS_X, ACROSS_Y, INNER):
+            self.describe(ref, link, self.recv.at[self.place.row, q]).start()
+
+        @pl.when(self.place.plane > 0)
+        def _():
+            self.describe(ref, OUTER, self.recv.at[self.place.row, q]).start()
+
+        self.describe(ref, PARTNER, self.met.at[q]).start()
+
+    def meet(self, q):
+        self.describe(self.own(q, 1 - self.place.col), PARTNER, self.met.at[q]).wait_recv()
+
+    def run(self, after, until):
+        for plane in self.near:
+            chosen = [act for act in self.acts[plane] if after < act[0] <= until]
+            if chosen:
+
+                @pl.when(self.place.plane == plane)
+                def _(chosen=chosen):
+                    for act in chosen:
+                        if act[1] == "take":
+                            self.copy(INNER, act[2]).wait_recv()
+                            self.copy(PARTNER, act[2]).start()
+                        else:
+                            self.copy(act[2], act[3]).start()
+
+    def all_passed(self):
+        count = (self.place.planes * CORNERS - 1) * self.parts * self.size
+        self.describe(self.all_ref.at[pl.ds(0, count)], PARTNER, self.passed).wait_recv()
+
+    def all_sent(self):
+        for plane in self.near:
+
+            @pl.when(self.place.plane == plane)
+            def _(plane=plane):
+                counts = [0] * 5
+                for act in self.acts[plane]:
+                    counts[PARTNER if act[1] == "take" else act[2]] += 1
+                for link in range(5):
+                    own = self.parts if link != OUTER or plane > 0 else 0
+                    total = (counts[link] + own) * self.size
+                    if total:
+                        ref = self.all_ref.at[pl.ds(0, total)]
+                        self.describe(ref, link, self.passed).wait_send()
+
+
+def greet(place):
+    barrier = pltpu.get_barrier_semaphore()
+    for link in (ACROSS_X, ACROSS_Y, PARTNER, INNER):
+        pl.semaphore_signal(barrier, inc=1, device_id=place.target[link], device_id_type=MESH)
+
+    @pl.when(place.plane > 0)
+    def _():
+        pl.semaphore_signal(barrier, inc=1, device_id=place.target[OUTER], device_id_type=MESH)
+
+    pl.semaphore_wait(barrier, 4 + (place.plane > 0).astype(jnp.int32))
 
 
 def slot_groups(slot_count):
@@ -382,6 +387,7 @@
     y_in,
     recv,
     passed,
+    met,
     sent,
     local,
     pair,
@@ -402,22 +408,35 @@
     take.start()
     load.start()
     load_diag.start()
+
+    def gather(n, all_ref, ready):
+        return Gather(
+            place, all_ref, diag_blocks, recv.at[n], passed.at[n], met.at[n], sent.at[n], ready
+        )
+
+    forever = float("inf")
+    gathers = [gather(0, x_all, [0.0] * diag_blocks)]
     greet(place)
     take.wait()
-    gather(place, x_all, recv.at[0], passed.at[0], sent)
+    for q in range(diag_blocks):
+        gathers[0].start_own(q)
+    gathers[0].run(-1.0, forever)
+    for q in range(diag_blocks):
+        gathers[0].meet(q)
+    gathers[0].all_passed()
     load.wait()
     load_diag.wait()
 
     def y_row(a):
         y_part[a] = product_row(lambda s: tiles[a, s], lambda s: x_all[pattern[a, s]], slot_count)
 
-    def send_partial(sweep):
+    def send_partial(sweep, d):
         return pltpu.make_async_remote_copy(
-            src_ref=y_part.at[pl.ds(first_other, diag_blocks)],
-            dst_ref=y_in.at[sweep],
-            send_sem=pair.at[0, sweep],
-            recv_sem=pair.at[1, sweep],
-            device_id=place.partner(),
+            src_ref=y_part.at[first_other + d],
+            dst_ref=y_in.at[sweep, d],
+            send_sem=pair.at[0, sweep, d],
+            recv_sem=pair.at[1, sweep, d],
+            device_id=place.target[PARTNER],
             device_id_type=MESH,
         )
 
@@ -442,46 +461,66 @@
         )
         diag[d] = stepped_diag(diag[d], pair_sum, sample_count)
 
-    def products(sweep, y_all, before):
+    def products(sweep, before):
+        y_all = y_every[sweep]
+        row_us = ROW_US[min(sweep, 1)]
+        ready = [2 * row_us * d for d in range(diag_blocks)]
+        going = gather(1 + sweep, y_all, ready)
+        gathers.append(going)
+
+        def finalize(d):
+            send_partial(sweep, d).wait()
+            y_all[first_own + first_diag + d] = y_part[first_diag + d] + y_in[sweep, d]
+            going.start_own(d)
+
         @pl.loop(0, diag_blocks)
         def _(d):
             before(first_other + d)
             y_row(first_other + d)
-
-        sending = send_partial(sweep)
-        sending.start()
-
-        @pl.loop(0, diag_blocks)
-        def _(d):
+            send_partial(sweep, d).start()
+
+            @pl.when(d > 0)
+            def _():
+                finalize(d - 1)
+
+            for k in range(1, diag_blocks):
+
+                @pl.when(d == k)
+                def _(k=k):
+                    going.run(ready[k - 1] - 2 * row_us, ready[k - 1])
+
             before(first_diag + d)
             y_row(first_diag + d)
             y_part[first_diag + d] += fold(times(diag[d], x_all[first_own + first_diag + d]))
 
-        sending.wait()
-
-        @pl.loop(0, diag_blocks)
-        def _(d):
-            y_all[first_own + first_diag + d] = y_part[first_diag + d] + y_in[sweep, d]
-
-        def unit(first):
-            @pl.loop(0, WORK_ROWS)
-            def _(n):
-                cross_tiles((first_diag + first + n) % block_rows, y_all)
-
-        def unit_diag():
-            @pl.loop(0, diag_blocks)
-            def _(d):
-                step_own(d, y_all)
-
-        work = [lambda first=first: unit(first) for first in range(0, block_rows, WORK_ROWS)]
-        work.insert(1, unit_diag)
-        gather(place, y_all, recv.at[1 + sweep], passed.at[1 + sweep], sent, work)
-
-    products(0, y_every[0], lambda a: None)
-    for sweep in range(ITERS - 1):
-        products(
-            sweep + 1, y_every[sweep + 1], lambda a: mirror_tiles(a, y_every[sweep])
-        )
+        finalize(diag_blocks - 1)
+
+        @pl.loop(0, block_rows)
+        def _(n):
+            for k in range(block_rows):
+
+                @pl.when(n == k)
+                def _(k=k):
+                    if k == diag_blocks:
+                        for q in range(diag_blocks):
+                            going.meet(q)
+                    begin = ready[-1] + k * UNIT_US
+                    going.run(ready[-2] if k == 0 else begin - UNIT_US, begin)
+
+            cross_tiles((first_diag + n) % block_rows, y_all)
+
+            @pl.when(n < diag_blocks)
+            def _():
+                step_own(n, y_all)
+
+        going.run(ready[-1] + (block_rows - 1) * UNIT_US, forever)
+        going.all_passed()
+
+    products(0, lambda a: None)
+    for sweep in range(1, ITERS):
+        products(sweep, lambda a: mirror_tiles(a, y_every[sweep - 1]))
+    for done in gathers:
+        done.all_sent()
 
 
 def finish_kernel(pattern, tiles, x_all, y_all, diag_in, tiles_out, diag_out, ready, sems):
@@ -527,11 +566,12 @@
         scratch_shapes=[
             pltpu.VMEM((block_rows, size, sample_count), jnp.float32),
             pltpu.VMEM((ITERS, diag_blocks, size, sample_count), jnp.float32),
-            pltpu.SemaphoreType.DMA((1 + ITERS, row_count, PARTS)),
-            pltpu.SemaphoreType.DMA((1 + ITERS, row_count, PARTS)),
-            pltpu.SemaphoreType.DMA((5, row_count, PARTS)),
+            pltpu.SemaphoreType.DMA((1 + ITERS, row_count, diag_blocks)),
+            pltpu.SemaphoreType.DMA((1 + ITERS,)),
+            pltpu.SemaphoreType.DMA((1 + ITERS, diag_blocks)),
+            pltpu.SemaphoreType.DMA((1 + ITERS, 5)),
             pltpu.SemaphoreType.DMA((3,)),
-            pltpu.SemaphoreType.DMA((2, ITERS)),
+            pltpu.SemaphoreType.DMA((2, ITERS, diag_blocks)),
         ]
         + [pltpu.VMEM(every, jnp.float32)] * (ITERS - 1),
         compiler_params=pltpu.CompilerParams(
@@ -568,7 +608,7 @@
     block_rows, slot_count = omega_tiles.shape[:2]
     peer_span = row_count // 2 - 2
     capacity = max(1, (slot_count * block_rows // 2 - 1 + peer_span - 1) // peer_span)
-    whole_gather = 2 * capacity >= block_rows and lax.axis_size("col") == 2 and row_count % 4 == 0
+    whole_gather = 2 * capacity >= block_rows and lax.axis_size("col") == 2 and row_count % 8 == 0
     sweeps = gathered_sweeps if whole_gather else listed_sweeps
     return sweeps(omega_tiles, omega_diag, samples, pattern)
 

time: 124 us -> 112 us (0.903)
  Pallas kernels: 123 us -> 111 us
    pallas_call x1, Pallas kernels: 118 us -> 105 us  [gathered_sweeps(): pl.pallas_call(sweeps_kernel, name='sweeps', out_shape=[pltpu.VMEM(omega_...]
where the time goes in v2:
time: 112 us; the launch traced here: 111 us
  Pallas kernels  111 us (99%)
    pallas_call x1, Pallas kernels, gathered_sweeps(): pl.pallas_call(sweeps_kernel, name='sweeps', out_shape=[pltpu.VMEM(omega_...  105 us
    pallas_call x1, Pallas kernels, gathered_sweeps(): pl.pallas_call(finish_kernel, name='finish', out_shape=[jax.ShapeDtypeStr...  5.64 us

profile of v2, /device:TPU:0, one launch (start us, length us, event | category | flops | bytes accessed | tf_op | source)
XLA Modules:
  0.0 111.4 jit_solution(15189601436720520181)
XLA Ops:
  0.6 0.0 copy-start
  0.6 105.1 %sweeps.1 = (f32[8,12,128,128]{3,2,1,0:T(8,128)S(1)}, f32[128,128,128]{2,1,0:T(8,128)S(1)}, f32[128,128,128]{2,1,0:T(8,128)S(1)}, f32[4,128,128]{2,1,0:T(8,128)S(1)}) custom-call(s32[8,12]{1,0:T(8,128)} %pattern.3, f32[8,12,128,128]{3,2,1,0:T(8,128)} %tiles_in.1, f32[4,128,128]{2,1,0:T(8,128)} %bitcast.3, f32[4,128,128]{2,1,0:T(8,128)} %bitcast.4), custom_call_target="tpu_custom_call" | custom-call | tf_op jit(solution)/shard_map/sweeps/pallas_call | solution.py:555
  105.7 0.0 copy-done
  105.8 5.6 %finish.1 = (f32[8,12,128,128]{3,2,1,0:T(8,128)}, f32[4,128,128]{2,1,0:T(8,128)}) custom-call(s32[8,12]{1,0:T(8,128)S(1)} %copy-done, f32[8,12,128,128]{3,2,1,0:T(8,128)S(1)} %get-tuple-element.8.tiles, f32[128,128,128]{2,1,0:T(8,128)S(1)} %get-tuple-element.9.x_all, f32[128,128,128]{2,1,0:T(8,128)S(1)} %get-tuple-element.10.y_all, ...), custom_call_target="tpu_custom_call" | custom-call | tf_op jit(solution)/shard_map/finish/pallas_call | solution.py:588
Async XLA Ops:
  0.6 105.1 %copy-start = (s32[8,12]{1,0:T(8,128)S(1)}, s32[8,12]{1,0:T(8,128)}, u32[]{:S(2)}) copy-start(s32[8,12]{1,0:T(8,128)} %pattern.3) | copy-start | bytes 1156

commit v3 on v2

--- a/solution.py
+++ b/solution.py
@@ -150,8 +150,8 @@
 SLOT_GROUP = 2
 SEND_US = 1.44
 HOP_US = 1.7
-LEAD_US = 1.5
-ROW_US = (0.55, 1.1)
+LEAD_US = 2.5
+ROW_US = (0.42, 0.85)
 UNIT_US = 1.44
 INNER, OUTER, ACROSS_X, ACROSS_Y, PARTNER = range(5)
 
@@ -375,7 +375,7 @@
 
 
 def sweeps_kernel(
-    pattern,
+    pattern_in,
     tiles_in,
     diag_in,
     samples,
@@ -383,6 +383,7 @@
     x_all,
     y_last,
     diag,
+    pattern,
     y_part,
     y_in,
     recv,
@@ -403,15 +404,17 @@
     first_other = (1 - place.col) * diag_blocks
     load = pltpu.make_async_copy(tiles_in, tiles, local.at[0])
     load_diag = pltpu.make_async_copy(diag_in, diag, local.at[2])
+    load_pattern = pltpu.make_async_copy(pattern_in, pattern, local.at[3])
     mine = pl.ds(first_own + first_diag, diag_blocks)
     take = pltpu.make_async_copy(samples, x_all.at[mine], local.at[1])
     take.start()
     load.start()
     load_diag.start()
+    load_pattern.start()
 
     def gather(n, all_ref, ready):
         return Gather(
-            place, all_ref, diag_blocks, recv.at[n], passed.at[n], met.at[n], sent.at[n], ready
+            place, all_ref, diag_blocks, recv.at[n % 2], passed.at[n % 2], met.at[n % 2], sent.at[n], ready
         )
 
     forever = float("inf")
@@ -426,6 +429,7 @@
     gathers[0].all_passed()
     load.wait()
     load_diag.wait()
+    load_pattern.wait()
 
     def y_row(a):
         y_part[a] = product_row(lambda s: tiles[a, s], lambda s: x_all[pattern[a, s]], slot_count)
@@ -479,9 +483,11 @@
             y_row(first_other + d)
             send_partial(sweep, d).start()
 
-            @pl.when(d > 0)
-            def _():
-                finalize(d - 1)
+            if sweep == 0:
+
+                @pl.when(d > 0)
+                def _():
+                    finalize(d - 1)
 
             for k in range(1, diag_blocks):
 
@@ -492,8 +498,11 @@
             before(first_diag + d)
             y_row(first_diag + d)
             y_part[first_diag + d] += fold(times(diag[d], x_all[first_own + first_diag + d]))
-
-        finalize(diag_blocks - 1)
+            if sweep:
+                finalize(d)
+
+        if sweep == 0:
+            finalize(diag_blocks - 1)
 
         @pl.loop(0, block_rows)
         def _(n):
@@ -527,7 +536,8 @@
     block_rows, slot_count = tiles.shape[:2]
     sample_count = x_all.shape[2]
     first_own = lax.axis_index("row") * block_rows
-    diag_out[...] = diag_in[...]
+    store_diag = pltpu.make_async_copy(diag_in, diag_out, sems.at[block_rows])
+    store_diag.start()
 
     def store(a):
         return pltpu.make_async_copy(ready.at[a], tiles_out.at[a], sems.at[a])
@@ -536,6 +546,8 @@
     def _(a):
         mirror_row(a, first_own, pattern, tiles, x_all, y_all, ready, sample_count)
         store(a).start()
+
+    store_diag.wait()
 
     @pl.loop(0, block_rows)
     def _(a):
@@ -552,7 +564,7 @@
     in_vmem = pl.BlockSpec(memory_space=pltpu.VMEM)
     in_hbm = pl.BlockSpec(memory_space=pltpu.HBM)
     in_smem = pl.BlockSpec(memory_space=pltpu.SMEM)
-    tiles, x_all, y_all, diag = pl.pallas_call(
+    tiles, x_all, y_all, diag, listed = pl.pallas_call(
         sweeps_kernel,
         name="sweeps",
         out_shape=[
@@ -560,17 +572,18 @@
             pltpu.VMEM(every, jnp.float32),
             pltpu.VMEM(every, jnp.float32),
             pltpu.VMEM(diag.shape, jnp.float32),
+            pltpu.SMEM(pattern.shape, jnp.int32),
         ],
-        in_specs=[in_smem, in_hbm, in_hbm, in_hbm],
-        out_specs=[in_vmem] * 4,
+        in_specs=[in_hbm] * 4,
+        out_specs=[in_vmem] * 4 + [in_smem],
         scratch_shapes=[
             pltpu.VMEM((block_rows, size, sample_count), jnp.float32),
             pltpu.VMEM((ITERS, diag_blocks, size, sample_count), jnp.float32),
-            pltpu.SemaphoreType.DMA((1 + ITERS, row_count, diag_blocks)),
-            pltpu.SemaphoreType.DMA((1 + ITERS,)),
-            pltpu.SemaphoreType.DMA((1 + ITERS, diag_blocks)),
+            pltpu.SemaphoreType.DMA((2, row_count, diag_blocks)),
+            pltpu.SemaphoreType.DMA((2,)),
+            pltpu.SemaphoreType.DMA((2, diag_blocks)),
             pltpu.SemaphoreType.DMA((1 + ITERS, 5)),
-            pltpu.SemaphoreType.DMA((3,)),
+            pltpu.SemaphoreType.DMA((4,)),
             pltpu.SemaphoreType.DMA((2, ITERS, diag_blocks)),
         ]
         + [pltpu.VMEM(every, jnp.float32)] * (ITERS - 1),
@@ -578,10 +591,9 @@
             collective_id=0, has_side_effects=True, vmem_limit_bytes=40 * 2**20
         ),
     )(
-        pattern,
         *(
             pltpu.with_memory_space_constraint(v, pltpu.HBM)
-            for v in (omega_tiles, diag, samples.reshape(diag_blocks, size, sample_count))
+            for v in (pattern, omega_tiles, diag, samples.reshape(diag_blocks, size, sample_count))
         ),
     )
     held = [pltpu.with_memory_space_constraint(v, pltpu.VMEM) for v in (tiles, x_all, y_all, diag)]
@@ -593,13 +605,13 @@
             jax.ShapeDtypeStruct(diag.shape, jnp.float32),
         ],
         in_specs=[in_smem] + [in_vmem] * 4,
-        out_specs=[in_hbm, in_vmem],
+        out_specs=[in_hbm, in_hbm],
         scratch_shapes=[
             pltpu.VMEM(omega_tiles.shape, jnp.float32),
-            pltpu.SemaphoreType.DMA((block_rows,)),
+            pltpu.SemaphoreType.DMA((block_rows + 1,)),
         ],
         compiler_params=pltpu.CompilerParams(vmem_limit_bytes=16 * 2**20),
-    )(pattern, *held)
+    )(pltpu.with_memory_space_constraint(listed, pltpu.SMEM), *held)
     return tiles, diag.reshape(omega_diag.shape)
 
 

time: 112 us -> 109 us (0.973)
  Pallas kernels: 111 us -> 108 us
    pallas_call x1, Pallas kernels: 105 us -> 103 us  [gathered_sweeps(): pl.pallas_call(sweeps_kernel, name='sweeps', out_shape=[pltpu.VMEM(omega_...]
    pallas_call x1, Pallas kernels: 5.64 us -> 4.34 us  [gathered_sweeps(): pl.pallas_call(finish_kernel, name='finish', out_shape=[jax.ShapeDtypeStr...]
where the time goes in v3:
time: 109 us; the launch traced here: 108 us
  Pallas kernels  108 us (99%)
    pallas_call x1, Pallas kernels, gathered_sweeps(): pl.pallas_call(sweeps_kernel, name='sweeps', out_shape=[pltpu.VMEM(omega_...  103 us
    pallas_call x1, Pallas kernels, gathered_sweeps(): pl.pallas_call(finish_kernel, name='finish', out_shape=[jax.ShapeDtypeStr...  4.34 us

profile of v3, /device:TPU:0, one launch (start us, length us, event | category | flops | bytes accessed | tf_op | source)
XLA Modules:
  0.0 108.4 jit_solution(7512886948679922729)
XLA Ops:
  0.6 103.4 %sweeps.1 = (f32[8,12,128,128]{3,2,1,0:T(8,128)S(1)}, f32[128,128,128]{2,1,0:T(8,128)S(1)}, f32[128,128,128]{2,1,0:T(8,128)S(1)}, f32[4,128,128]{2,1,0:T(8,128)S(1)}, s32[8,12]{1,0:T(8,128)S(4)}) custom-call(s32[8,12]{1,0:T(8,128)} %pattern_in.1, f32[8,12,128,128]{3,2,1,0:T(8,128)} %tiles_in.1, f32[4,128,128]{2,1,0:T(8,128)} %bitcast.3, f32[4,128,128]{2,1,0:T(8,128)} %bitcast.4), custom_call_target="tpu_custom_call" | custom-call | tf_op jit(solution)/shard_map/sweeps/pallas_call | solution.py:567
  104.1 4.3 %finish.1 = (f32[8,12,128,128]{3,2,1,0:T(8,128)}, f32[4,128,128]{2,1,0:T(8,128)}) custom-call(s32[8,12]{1,0:T(8,128)S(4)} %get-tuple-element.9.pattern, f32[8,12,128,128]{3,2,1,0:T(8,128)S(1)} %get-tuple-element.10.tiles, f32[128,128,128]{2,1,0:T(8,128)S(1)} %get-tuple-element.11.x_all, f32[128,128,128]{2,1,0:T(8,128)S(1)} %get-tuple-element.12.y_all, ...), custom_call_target="tpu_custom_call" | custom-call | tf_op jit(solution)/shard_map/finish/pallas_call | solution.py:600

commit v4 on v3

--- a/solution.py
+++ b/solution.py
@@ -542,10 +542,12 @@
     def store(a):
         return pltpu.make_async_copy(ready.at[a], tiles_out.at[a], sems.at[a])
 
-    @pl.loop(0, block_rows)
-    def _(a):
-        mirror_row(a, first_own, pattern, tiles, x_all, y_all, ready, sample_count)
-        store(a).start()
+    def rows(first):
+        for a in (first, first + 1):
+            mirror_row(a, first_own, pattern, tiles, x_all, y_all, ready, sample_count)
+            store(a).start()
+
+    pl.loop(0, block_rows, step=2)(rows)
 
     store_diag.wait()
 

time: 109 us -> 108 us (level)
  no operation moved by 1% of the time
where the time goes in v4:
time: 108 us
  Pallas kernels  107 us (99%)
    pallas_call x1, Pallas kernels, gathered_sweeps(): pl.pallas_call(sweeps_kernel, name='sweeps', out_shape=[pltpu.VMEM(omega_...  103 us
    pallas_call x1, Pallas kernels, gathered_sweeps(): pl.pallas_call(finish_kernel, name='finish', out_shape=[jax.ShapeDtypeStr...  3.58 us

profile of v4, /device:TPU:0, one launch (start us, length us, event | category | flops | bytes accessed | tf_op | source)
XLA Modules:
  0.0 107.6 jit_solution(6922224239163796863)
XLA Ops:
  0.6 103.4 %sweeps.1 = (f32[8,12,128,128]{3,2,1,0:T(8,128)S(1)}, f32[128,128,128]{2,1,0:T(8,128)S(1)}, f32[128,128,128]{2,1,0:T(8,128)S(1)}, f32[4,128,128]{2,1,0:T(8,128)S(1)}, s32[8,12]{1,0:T(8,128)S(4)}) custom-call(s32[8,12]{1,0:T(8,128)} %pattern_in.1, f32[8,12,128,128]{3,2,1,0:T(8,128)} %tiles_in.1, f32[4,128,128]{2,1,0:T(8,128)} %bitcast.3, f32[4,128,128]{2,1,0:T(8,128)} %bitcast.4), custom_call_target="tpu_custom_call" | custom-call | tf_op jit(solution)/shard_map/sweeps/pallas_call | solution.py:569
  104.1 3.6 %finish.1 = (f32[8,12,128,128]{3,2,1,0:T(8,128)}, f32[4,128,128]{2,1,0:T(8,128)}) custom-call(s32[8,12]{1,0:T(8,128)S(4)} %get-tuple-element.9.pattern, f32[8,12,128,128]{3,2,1,0:T(8,128)S(1)} %get-tuple-element.10.tiles, f32[128,128,128]{2,1,0:T(8,128)S(1)} %get-tuple-element.11.x_all, f32[128,128,128]{2,1,0:T(8,128)S(1)} %get-tuple-element.12.y_all, ...), custom_call_target="tpu_custom_call" | custom-call | tf_op jit(solution)/shard_map/finish/pallas_call | solution.py:602

commit v5 on v4

--- a/solution.py
+++ b/solution.py
@@ -346,7 +346,7 @@
                         self.describe(ref, link, self.passed).wait_send()
 
 
-def greet(place):
+def greet(place, meanwhile):
     barrier = pltpu.get_barrier_semaphore()
     for link in (ACROSS_X, ACROSS_Y, PARTNER, INNER):
         pl.semaphore_signal(barrier, inc=1, device_id=place.target[link], device_id_type=MESH)
@@ -355,6 +355,7 @@
     def _():
         pl.semaphore_signal(barrier, inc=1, device_id=place.target[OUTER], device_id_type=MESH)
 
+    meanwhile()
     pl.semaphore_wait(barrier, 4 + (place.plane > 0).astype(jnp.int32))
 
 
@@ -407,19 +408,20 @@
     load_pattern = pltpu.make_async_copy(pattern_in, pattern, local.at[3])
     mine = pl.ds(first_own + first_diag, diag_blocks)
     take = pltpu.make_async_copy(samples, x_all.at[mine], local.at[1])
-    take.start()
-    load.start()
-    load_diag.start()
-    load_pattern.start()
 
     def gather(n, all_ref, ready):
         return Gather(
-            place, all_ref, diag_blocks, recv.at[n % 2], passed.at[n % 2], met.at[n % 2], sent.at[n], ready
+            place, all_ref, diag_blocks, recv.at[n % 2], passed.at[n % 2], met.at[n % 2], sent.at[n % 2], ready
         )
 
     forever = float("inf")
     gathers = [gather(0, x_all, [0.0] * diag_blocks)]
-    greet(place)
+
+    def start_loads():
+        for copy in (take, load_pattern, load, load_diag):
+            copy.start()
+
+    greet(place, start_loads)
     take.wait()
     for q in range(diag_blocks):
         gathers[0].start_own(q)
@@ -438,8 +440,8 @@
         return pltpu.make_async_remote_copy(
             src_ref=y_part.at[first_other + d],
             dst_ref=y_in.at[sweep, d],
-            send_sem=pair.at[0, sweep, d],
-            recv_sem=pair.at[1, sweep, d],
+            send_sem=pair.at[0, d],
+            recv_sem=pair.at[1, d],
             device_id=place.target[PARTNER],
             device_id_type=MESH,
         )
@@ -522,14 +524,14 @@
             def _():
                 step_own(n, y_all)
 
+        gathers[sweep].all_sent()
         going.run(ready[-1] + (block_rows - 1) * UNIT_US, forever)
         going.all_passed()
 
     products(0, lambda a: None)
     for sweep in range(1, ITERS):
         products(sweep, lambda a: mirror_tiles(a, y_every[sweep - 1]))
-    for done in gathers:
-        done.all_sent()
+    gathers[-1].all_sent()
 
 
 def finish_kernel(pattern, tiles, x_all, y_all, diag_in, tiles_out, diag_out, ready, sems):
@@ -584,9 +586,9 @@
             pltpu.SemaphoreType.DMA((2, row_count, diag_blocks)),
             pltpu.SemaphoreType.DMA((2,)),
             pltpu.SemaphoreType.DMA((2, diag_blocks)),
-            pltpu.SemaphoreType.DMA((1 + ITERS, 5)),
+            pltpu.SemaphoreType.DMA((2, 5)),
             pltpu.SemaphoreType.DMA((4,)),
-            pltpu.SemaphoreType.DMA((2, ITERS, diag_blocks)),
+            pltpu.SemaphoreType.DMA((2, diag_blocks)),
         ]
         + [pltpu.VMEM(every, jnp.float32)] * (ITERS - 1),
         compiler_params=pltpu.CompilerParams(

time: 108 us -> 108 us (level)
  no operation moved by 1% of the time
where the time goes in v5:
time: 108 us
  Pallas kernels  107 us (99%)
    pallas_call x1, Pallas kernels, gathered_sweeps(): pl.pallas_call(sweeps_kernel, name='sweeps', out_shape=[pltpu.VMEM(omega_...  103 us
    pallas_call x1, Pallas kernels, gathered_sweeps(): pl.pallas_call(finish_kernel, name='finish', out_shape=[jax.ShapeDtypeStr...  3.58 us

profile of v5, /device:TPU:0, one launch (start us, length us, event | category | flops | bytes accessed | tf_op | source)
XLA Modules:
  0.0 107.5 jit_solution(2456143586289225366)
XLA Ops:
  0.6 103.3 %sweeps.1 = (f32[8,12,128,128]{3,2,1,0:T(8,128)S(1)}, f32[128,128,128]{2,1,0:T(8,128)S(1)}, f32[128,128,128]{2,1,0:T(8,128)S(1)}, f32[4,128,128]{2,1,0:T(8,128)S(1)}, s32[8,12]{1,0:T(8,128)S(4)}) custom-call(s32[8,12]{1,0:T(8,128)} %pattern_in.1, f32[8,12,128,128]{3,2,1,0:T(8,128)} %tiles_in.1, f32[4,128,128]{2,1,0:T(8,128)} %bitcast.3, f32[4,128,128]{2,1,0:T(8,128)} %bitcast.4), custom_call_target="tpu_custom_call" | custom-call | tf_op jit(solution)/shard_map/sweeps/pallas_call | solution.py:571
  103.9 3.6 %finish.1 = (f32[8,12,128,128]{3,2,1,0:T(8,128)}, f32[4,128,128]{2,1,0:T(8,128)}) custom-call(s32[8,12]{1,0:T(8,128)S(4)} %get-tuple-element.9.pattern, f32[8,12,128,128]{3,2,1,0:T(8,128)S(1)} %get-tuple-element.10.tiles, f32[128,128,128]{2,1,0:T(8,128)S(1)} %get-tuple-element.11.x_all, f32[128,128,128]{2,1,0:T(8,128)S(1)} %get-tuple-element.12.y_all, ...), custom_call_target="tpu_custom_call" | custom-call | tf_op jit(solution)/shard_map/finish/pallas_call | solution.py:604

commit v6 on v5

--- a/solution.py
+++ b/solution.py
@@ -544,12 +544,14 @@
     def store(a):
         return pltpu.make_async_copy(ready.at[a], tiles_out.at[a], sems.at[a])
 
-    def rows(first):
-        for a in (first, first + 1):
+    def rows(first, count):
+        for a in range(first, first + count):
             mirror_row(a, first_own, pattern, tiles, x_all, y_all, ready, sample_count)
             store(a).start()
 
-    pl.loop(0, block_rows, step=2)(rows)
+    rows(0, block_rows // 2)
+    rows(block_rows // 2, block_rows // 4)
+    rows(block_rows // 2 + block_rows // 4, block_rows - block_rows // 2 - block_rows // 4)
 
     store_diag.wait()
 

time: 108 us -> 107 us (level)
  no operation moved by 1% of the time
where the time goes in v6:
time: 107 us
  Pallas kernels  106 us (99%)
    pallas_call x1, Pallas kernels, gathered_sweeps(): pl.pallas_call(sweeps_kernel, name='sweeps', out_shape=[pltpu.VMEM(omega_...  103 us
    pallas_call x1, Pallas kernels, gathered_sweeps(): pl.pallas_call(finish_kernel, name='finish', out_shape=[jax.ShapeDtypeStr...  3.16 us

profile of v6, /device:TPU:0, one launch (start us, length us, event | category | flops | bytes accessed | tf_op | source)
XLA Modules:
  0.0 107.1 jit_solution(2389226304725514229)
XLA Ops:
  0.6 103.3 %sweeps.1 = (f32[8,12,128,128]{3,2,1,0:T(8,128)S(1)}, f32[128,128,128]{2,1,0:T(8,128)S(1)}, f32[128,128,128]{2,1,0:T(8,128)S(1)}, f32[4,128,128]{2,1,0:T(8,128)S(1)}, s32[8,12]{1,0:T(8,128)S(4)}) custom-call(s32[8,12]{1,0:T(8,128)} %pattern_in.1, f32[8,12,128,128]{3,2,1,0:T(8,128)} %tiles_in.1, f32[4,128,128]{2,1,0:T(8,128)} %bitcast.3, f32[4,128,128]{2,1,0:T(8,128)} %bitcast.4), custom_call_target="tpu_custom_call" | custom-call | tf_op jit(solution)/shard_map/sweeps/pallas_call | solution.py:573
  103.9 3.2 %finish.1 = (f32[8,12,128,128]{3,2,1,0:T(8,128)}, f32[4,128,128]{2,1,0:T(8,128)}) custom-call(s32[8,12]{1,0:T(8,128)S(4)} %get-tuple-element.9.pattern, f32[8,12,128,128]{3,2,1,0:T(8,128)S(1)} %get-tuple-element.10.tiles, f32[128,128,128]{2,1,0:T(8,128)S(1)} %get-tuple-element.11.x_all, f32[128,128,128]{2,1,0:T(8,128)S(1)} %get-tuple-element.12.y_all, ...), custom_call_target="tpu_custom_call" | custom-call | tf_op jit(solution)/shard_map/finish/pallas_call | solution.py:606
